TPU v7x, 32 devices: a whole 2x2x4 slice. The times are simulated.
32 devices in a mesh: grp: 2 (over y), scen: 4 (over z), blk: 2 (over x), sub: 2 (over core).
Axes of the slice: x: 2, y: 2, z: 4, core: 2. Of those that a mesh axis runs over, the one named last changes fastest.
Arguments:
- block_matrices: float32 [8, 256, 128, 128], P(('grp', 'scen'), ('blk', 'sub')), parts along dimension 0, may hold values from -0.25 to 0.25
- slot_row_block: int32 [8, 256], P(('grp', 'scen'), ('blk', 'sub')), parts along dimension 0, may hold values from 0 to 7
- tile_column: int32 [8, 256], P(('grp', 'scen'), ('blk', 'sub')), parts along dimension 0, may hold values from 0 to 4127, as said below
- block_count: int32 [8, 4], P(('grp', 'scen'), ('blk', 'sub')), parts along dimension 0, may hold values from 8 to 64, as said below
- carbon_scenario: int32 [8], P(('grp', 'scen')), parts along dimension 0, may hold values from 0 to 23
- intensity: float32 [24, 32, 128], P(None, ('blk', 'sub')), may hold values from 0.2 to 2
- cost_first: float32 [8192, 128], P(('grp', 'scen', 'blk', 'sub')), parts along dimension 0, may hold values from -6 to 6
- lower_first: float32 [8192, 128], P(('grp', 'scen', 'blk', 'sub')), parts along dimension 0, may hold values from -1 to -0.2
- upper_first: float32 [8192, 128], P(('grp', 'scen', 'blk', 'sub')), parts along dimension 0, may hold values from 0.2 to 1
- cost_second: float32 [8, 32, 128], P(('grp', 'scen'), ('blk', 'sub')), parts along dimension 0, may hold values from -6 to 6
- upper_second: float32 [8, 32, 128], P(('grp', 'scen'), ('blk', 'sub')), parts along dimension 0, may hold values from 0.2 to 2
- row_bound: float32 [8, 32, 128], P(('grp', 'scen'), ('blk', 'sub')), parts along dimension 0, may hold values from -20 to 20
- first_start: float32 [8192, 128], P(('grp', 'scen', 'blk', 'sub')), parts along dimension 0, may hold values from -0.2 to 0.2
- second_start: float32 [8, 32, 128], P(('grp', 'scen'), ('blk', 'sub')), parts along dimension 0, may hold values from 0 to 0.2
- dual_start: float32 [8, 32, 128], P(('grp', 'scen'), ('blk', 'sub')), parts along dimension 0, may hold values from 0 to 1
Outputs:
- first_final: float32 [8192, 128], P(('grp', 'scen', 'blk', 'sub')), parts along dimension 0
- second_final: float32 [8, 32, 128], P(('grp', 'scen'), ('blk', 'sub')), parts along dimension 0
- dual_final: float32 [8, 32, 128], P(('grp', 'scen'), ('blk', 'sub')), parts along dimension 0
- residual_norm: float32 [6], P('grp'), parts along dimension 0
There are 2 independent parts, one for each index of `grp`. A program takes and returns all parts, laid end to end along the dimension named above; an argument that names none is the same for every part. Nothing has to cross between parts.
Inputs may be any that keep to these rules, and one draw needn't show every extreme that they name: `block_count`: each scenario has one index of blk and sub with all 64 slots used; the others use between 8 and 32. `tile_column`: values below 4096 name first-section column blocks, values from 4096 on second-section ones. Split the first-section blocks into 16 equal shards in order, and take the slots of one index of scen and of blk and sub together (64 of them, scenario by scenario). In every draw, on every such device, at most 4 of them name first-section blocks of one shard, and some shard is named by exactly 4.
All inputs are finite; a program needn't handle non-finite values.
Results may differ from a plain program's by a relative error of at most 0.0003.
Values sent between devices are 32-bit elements; how exact they have to be, the bound alone decides.
No kernel may reach another device: no remote copies, remote signals or barrier semaphores. Data moves between devices by JAX's collectives and lax.ppermute only.
A program may use at most 64 MiB of HBM per device.

v0:
```python
import jax
import jax.numpy as jnp
from jax import lax
from jax.sharding import PartitionSpec as P

ITERS = 3
precise = lax.Precision.HIGHEST
step_primal = 0.4
step_dual = 0.4


def forward_window(
    block_matrices,
    onehot,
    mask,
    tile_column,
    fetch_first,
    count_first,
    second_bar,
    offset,
    window_size,
):
    count_second = second_bar.shape[1]
    is_first = tile_column < count_first
    from_first = fetch_first(tile_column, offset, window_size)
    second_index = jnp.clip(tile_column - count_first, 0, count_second - 1)
    from_second = jax.vmap(lambda table, index: table[index])(second_bar, second_index)
    blocks = jnp.where(is_first[:, :, None], from_first, from_second)
    product = jnp.einsum("skij,skj->ski", block_matrices, blocks, precision=precise)
    product = product * mask[:, :, None]
    return jnp.einsum("skr,ski->sri", onehot, product, precision=precise)


def adjoint_window(
    block_matrices,
    onehot,
    mask,
    tile_column,
    dual,
    collect_first,
    count_first,
    count_second,
    offset,
    window_size,
):
    gathered = jnp.einsum("skr,sri->ski", onehot, dual, precision=precise)
    product = jnp.einsum("skij,ski->skj", block_matrices, gathered, precision=precise)
    product = product * mask[:, :, None]
    is_first = tile_column < count_first
    first_terms = collect_first(product, tile_column, offset, window_size)
    second_index = jnp.where(is_first, count_second, tile_column - count_first)
    scenario_index = lax.broadcasted_iota(jnp.int32, second_index.shape, 0)
    second_terms = (
        jnp.zeros((product.shape[0], count_second, product.shape[2]), jnp.float32)
        .at[scenario_index, second_index]
        .add(product, mode="drop")
    )
    return (first_terms, second_terms)


def shards(
    block_matrices,
    slot_row_block,
    tile_column,
    block_count,
    carbon_scenario,
    intensity,
    cost_first,
    lower_first,
    upper_first,
    cost_second,
    upper_second,
    row_bound,
    first_start,
    second_start,
    dual_start,
):
    scen_local, slots = slot_row_block.shape
    rows_local = row_bound.shape[1]
    tile_size = row_bound.shape[2]
    shard_first = cost_first.shape[0]
    owner_count = lax.axis_size(("scen", "blk", "sub"))
    count_first = shard_first * owner_count
    count_second = cost_second.shape[1] * lax.axis_size(("blk", "sub"))
    total_cells = scen_local * rows_local * tile_size * owner_count
    mask = (jnp.arange(slots, dtype=jnp.int32)[None, :] < block_count).astype(jnp.float32)
    onehot = (
        slot_row_block[:, :, None] == jnp.arange(rows_local, dtype=jnp.int32)[None, None, :]
    ).astype(jnp.float32)
    choose = (
        carbon_scenario[:, None] == jnp.arange(intensity.shape[0], dtype=jnp.int32)[None, :]
    ).astype(jnp.float32)
    cost_total = cost_second + jnp.einsum("sc,cbt->sbt", choose, intensity, precision=precise)
    first_shape = (count_first, tile_size)

    def collect_first(product, column_window, offset, width):
        first_index = jnp.where(column_window < count_first, column_window, count_first).reshape(-1)
        return (
            jnp.zeros(first_shape, jnp.float32)
            .at[first_index]
            .add(product.reshape(-1, tile_size), mode="drop")
        )

    def make_fetch(first_source):

        def fetch_first(column_window, offset, width):
            return first_source[jnp.clip(column_window, 0, count_first - 1)]

        return fetch_first

    cost_all, lower_all, upper_all, first_now = (
        lax.all_gather(cost_first, ("scen", "blk", "sub"), axis=0, tiled=True),
        lax.all_gather(lower_first, ("scen", "blk", "sub"), axis=0, tiled=True),
        lax.all_gather(upper_first, ("scen", "blk", "sub"), axis=0, tiled=True),
        lax.all_gather(first_start, ("scen", "blk", "sub"), axis=0, tiled=True),
    )
    second_now = second_start
    dual = dual_start
    squares = []
    for step_index in range(ITERS):
        grad_first_part, grad_second_part = adjoint_window(
            block_matrices,
            onehot,
            mask,
            tile_column,
            dual,
            collect_first,
            count_first,
            count_second,
            0,
            slots,
        )
        grad_second = lax.psum_scatter(
            grad_second_part, ("blk", "sub"), scatter_dimension=1, tiled=True
        )
        grad_first = lax.psum(grad_first_part, ("scen", "blk", "sub"))
        first_next = jnp.clip(
            first_now - step_primal * (cost_all - grad_first), lower_all, upper_all
        )
        first_source = 2.0 * first_next - first_now
        second_next = jnp.clip(
            second_now - step_primal * (cost_total - grad_second), 0.0, upper_second
        )
        second_bar = lax.all_gather(
            2.0 * second_next - second_now, ("blk", "sub"), axis=1, tiled=True
        )
        residual = row_bound - forward_window(
            block_matrices,
            onehot,
            mask,
            tile_column,
            make_fetch(first_source),
            count_first,
            second_bar,
            0,
            slots,
        )
        local_square = jnp.sum(residual * residual)
        squares.append(lax.psum(local_square, ("scen", "blk", "sub")))
        dual = jnp.maximum(dual + step_dual * residual, 0.0)
        first_now = first_next
        second_now = second_next
    totals = jnp.stack(squares)
    residual_norm = jnp.sqrt(totals / total_cells)
    offset = lax.axis_index(("scen", "blk", "sub")) * shard_first
    first_final = lax.dynamic_slice_in_dim(first_now, offset, shard_first, 0)
    return (first_final, second_now, dual, residual_norm)


def solution(mesh):
    return jax.shard_map(
        shards,
        mesh=mesh,
        in_specs=(
            P(("grp", "scen"), ("blk", "sub"), None, None),
            P(("grp", "scen"), ("blk", "sub")),
            P(("grp", "scen"), ("blk", "sub")),
            P(("grp", "scen"), ("blk", "sub")),
            P(("grp", "scen")),
            P(None, ("blk", "sub"), None),
            P(("grp", "scen", "blk", "sub"), None),
            P(("grp", "scen", "blk", "sub"), None),
            P(("grp", "scen", "blk", "sub"), None),
            P(("grp", "scen"), ("blk", "sub"), None),
            P(("grp", "scen"), ("blk", "sub"), None),
            P(("grp", "scen"), ("blk", "sub"), None),
            P(("grp", "scen", "blk", "sub"), None),
            P(("grp", "scen"), ("blk", "sub"), None),
            P(("grp", "scen"), ("blk", "sub"), None),
        ),
        out_specs=(
            P(("grp", "scen", "blk", "sub"), None),
            P(("grp", "scen"), ("blk", "sub"), None),
            P(("grp", "scen"), ("blk", "sub"), None),
            P("grp"),
        ),
        check_vma=False,
    )
```

profile of v0, /device:TPU:0, one launch (start us, length us, event | category | flops | bytes accessed | tf_op | source)
XLA Modules:
  0.0 587.6 jit_solution(10443737884723280404)
XLA Ops:
  9.5 5.3 fusion.10
  22.7 13.2 %all-reduce.1 = f32[1,32,128]{2,1,0:T(8,128)S(1)} all-reduce(f32[1,32,128]{2,1,0:T(8,128)S(1)} %bitcast.135), channel_id=2, replica_groups=mesh['grp'=2,'scen'=4,'blk'=2,'sub'=2] {'blk','sub'}, use_global_device_ids=true, to_apply=%region_3.4.clone | all-reduce | flops 4096 | bytes 32768
  36.1 5.2 all_gather.25
  42.1 75.8 %all-reduce.9.cloned.1.call-done = f32[4096,128]{1,0:T(8,128)} async-done(((f32[4096,128]{1,0:T(8,128)}), f32[4096,128]{1,0:T(8,128)}) %all-reduce.9.cloned.1.call-update) | async-done | bytes 2097168 | tf_op jit(solution)/shard_map/psum | solution.py:136
  117.9 43.1 %all-gather.11.cloned.1.call-done = f32[4096,128]{1,0:T(8,128)} async-done(((f32[256,128]{1,0:T(8,128)}), f32[4096,128]{1,0:T(8,128)}) %all-gather.11.cloned.1.call-update) | async-done | bytes 2097168 | tf_op jit(solution)/shard_map/all_gather | solution.py:112
  160.9 42.6 %all-gather.5.cloned.1.call-done = f32[4096,128]{1,0:T(8,128)} async-done(((f32[256,128]{1,0:T(8,128)}), f32[4096,128]{1,0:T(8,128)}) %all-gather.5.cloned.1.call-update) | async-done | bytes 2097168 | tf_op jit(solution)/shard_map/all_gather | solution.py:114
  203.6 42.5 %all-gather.7.cloned.1.call-done = f32[4096,128]{1,0:T(8,128)} async-done(((f32[256,128]{1,0:T(8,128)}), f32[4096,128]{1,0:T(8,128)}) %all-gather.7.cloned.1.call-update) | async-done | bytes 2097168 | tf_op jit(solution)/shard_map/all_gather | solution.py:113
  246.0 42.4 %all-gather.9.cloned.1.call-done = f32[4096,128]{1,0:T(8,128)} async-done(((f32[256,128]{1,0:T(8,128)}), f32[4096,128]{1,0:T(8,128)}) %all-gather.9.cloned.1.call-update) | async-done | bytes 2097168 | tf_op jit(solution)/shard_map/all_gather | solution.py:115
  288.5 5.9 %multiply_subtract_fusion.2 = (f32[4096,128]{1,0:T(8,128)S(1)}, f32[4096,128]{1,0:T(8,128)}) fusion(f32[4096,128]{1,0:T(8,128)} %all-gather.9.cloned.1.call-done, f32[4096,128]{1,0:T(8,128)} %all-gather.5.cloned.1.call-done, f32[4096,128]{1,0:T(8,128)} %all-gather.7.cloned.1.call-done, f32[4096,128]{1,0:T(8,128)} %all-gather.11.cloned.1.call-done, ...), kind=kLoop, calls=%fused_computation.28 | loop fusion | flops 3670016 | bytes 14680064 | tf_op jit(solution)/shard_map/sub | solution.py:140
  295.1 8.5 %fusion.8 = f32[64,1,128]{2,1,0:T(1,128)S(1)} fusion(f32[64,128,1]{1,2,0:T(1,128)S(1)} %bitcast.130, f32[1,64,128,128]{3,2,1,0:T(8,128)} %param.15), kind=kOutput, calls=%fused_computation.20 | convolution fusion | flops 12582912 | bytes 4259840 | tf_op jit(solution)/shard_map/skij,skj->ski/dot_general | solution.py:29
  304.1 3.7 fusion.6
  311.0 10.4 %all-reduce.2 = f32[1,32,128]{2,1,0:T(8,128)S(1)} all-reduce(f32[1,32,128]{2,1,0:T(8,128)S(1)} %bitcast.137), channel_id=3, replica_groups=mesh['grp'=2,'scen'=4,'blk'=2,'sub'=2] {'blk','sub'}, use_global_device_ids=true, to_apply=%region_7.8.clone | all-reduce | flops 4096 | bytes 32768
  321.4 5.4 all_gather.26
  327.5 79.2 %all-reduce.11.cloned.1.call-done = f32[4096,128]{1,0:T(8,128)} async-done(((f32[4096,128]{1,0:T(8,128)}), f32[4096,128]{1,0:T(8,128)}) %all-reduce.11.cloned.1.call-update) | async-done | bytes 2097168 | tf_op jit(solution)/shard_map/psum | solution.py:136
  406.7 6.2 %multiply_subtract_fusion.1 = (f32[4096,128]{1,0:T(8,128)}, f32[4096,128]{1,0:T(8,128)}) fusion(f32[4096,128]{1,0:T(8,128)} %get-tuple-element.19, f32[4096,128]{1,0:T(8,128)} %all-gather.5.cloned.1.call-done, f32[4096,128]{1,0:T(8,128)} %all-gather.7.cloned.1.call-done, f32[4096,128]{1,0:T(8,128)S(1)} %copy-done.3, f32[4096,128]{1,0:T(8,128)} %all-reduce.11.cloned.1.call-done), kind=kLoop, calls=%fused_computation.26 | loop fusion | flops 3670016 | bytes 14680064 | tf_op jit(solution)/shard_map/sub | solution.py:140
  415.2 8.5 %fusion.4 = f32[64,1,128]{2,1,0:T(1,128)S(1)} fusion(f32[64,128,1]{1,2,0:T(1,128)S(1)} %bitcast.131, f32[1,64,128,128]{3,2,1,0:T(8,128)} %param.15), kind=kOutput, calls=%fused_computation.16 | convolution fusion | flops 12582912 | bytes 4259840 | tf_op jit(solution)/shard_map/skij,skj->ski/dot_general | solution.py:29
  424.2 3.7 fusion.2
  431.0 10.6 %all-reduce.3 = f32[1,32,128]{2,1,0:T(8,128)S(1)} all-reduce(f32[1,32,128]{2,1,0:T(8,128)S(1)} %bitcast.136), channel_id=4, replica_groups=mesh['grp'=2,'scen'=4,'blk'=2,'sub'=2] {'blk','sub'}, use_global_device_ids=true, to_apply=%region_11.12.clone | all-reduce | flops 4096 | bytes 32768
  442.2 5.4 all_gather.27
  448.4 79.0 %all-reduce.13.cloned.1.call-done = f32[4096,128]{1,0:T(8,128)} async-done(((f32[4096,128]{1,0:T(8,128)}), f32[4096,128]{1,0:T(8,128)}) %all-reduce.13.cloned.1.call-update) | async-done | bytes 2097168 | tf_op jit(solution)/shard_map/psum | solution.py:136
  527.3 6.2 %multiply_subtract_fusion = (f32[4096,128]{1,0:T(8,128)}, f32[4096,128]{1,0:T(8,128)}) fusion(f32[4096,128]{1,0:T(8,128)} %get-tuple-element.14, f32[4096,128]{1,0:T(8,128)} %all-gather.5.cloned.1.call-done, f32[4096,128]{1,0:T(8,128)} %all-gather.7.cloned.1.call-done, f32[4096,128]{1,0:T(8,128)S(1)} %copy-done.3, f32[4096,128]{1,0:T(8,128)} %all-reduce.13.cloned.1.call-done), kind=kLoop, calls=%fused_computation.24 | loop fusion | flops 3670016 | bytes 14680064 | tf_op jit(solution)/shard_map/sub | solution.py:140
  535.8 8.3 %fusion = f32[64,1,128]{2,1,0:T(1,128)S(1)} fusion(f32[64,128,1]{1,2,0:T(1,128)S(1)} %bitcast.129, f32[1,64,128,128]{3,2,1,0:T(8,128)} %param.15), kind=kOutput, calls=%fused_computation.12 | convolution fusion | flops 12582912 | bytes 4259840 | tf_op jit(solution)/shard_map/skij,skj->ski/dot_general | solution.py:29
  547.2 31.1 %all-reduce.4 = (f32[1]{0:T(128)}, f32[1]{0:T(128)}, f32[1]{0:T(128)}) all-reduce(f32[1]{0:T(128)} %bitcast.54, f32[1]{0:T(128)} %bitcast.53, f32[1]{0:T(128)} %bitcast.52), channel_id=1, replica_groups=mesh['grp'=2,'scen'=4,'blk'=2,'sub'=2] {'scen','blk','sub'}, use_global_device_ids=true, to_apply=%region_17.18 | all-reduce | flops 3 | bytes 24 | tf_op jit(solution)/shard_map/psum | solution.py:159
  578.3 2.5 fusion.82
  (74 shorter events, 27.0 us)
Async XLA Ops:
  7.2 28.7 %copy-start = (f32[24,8,128]{2,1,0:T(8,128)S(1)}, f32[24,8,128]{2,1,0:T(8,128)}, u32[]{:S(2)}) copy-start(f32[24,8,128]{2,1,0:T(8,128)} %param.20) | copy-start | bytes 294916
  7.2 110.7 %all-reduce.9.cloned.1.call-start = ((), (), s32[]{:S(2)}) async-start(), calls=%async_computation.4 | async-start | bytes 4194304 | tf_op jit(solution)/shard_map/psum | solution.py:136
  14.8 5.1 copy-start.9
  14.8 6.7 %copy-start.11 = (u32[32]{0:T(128)S(1)}, u32[32]{0:T(128)}, u32[]{:S(2)}) copy-start(u32[32]{0:T(128)} %constant.109) | copy-start | bytes 388
  14.8 21.3 %copy-start.4 = (f32[1,8,128]{2,1,0:T(8,128)S(1)}, f32[1,8,128]{2,1,0:T(8,128)}, u32[]{:S(2)}) copy-start(f32[1,8,128]{2,1,0:T(8,128)} %param.25) | copy-start | bytes 12292
  14.8 21.3 %copy-start.7 = (f32[1,8,128]{2,1,0:T(8,128)S(1)}, f32[1,8,128]{2,1,0:T(8,128)}, u32[]{:S(2)}) copy-start(f32[1,8,128]{2,1,0:T(8,128)} %param.28) | copy-start | bytes 12292
  14.8 21.3 %copy-start.8 = (f32[1,8,128]{2,1,0:T(8,128)S(1)}, f32[1,8,128]{2,1,0:T(8,128)}, u32[]{:S(2)}) copy-start(f32[1,8,128]{2,1,0:T(8,128)} %param.24) | copy-start | bytes 12292
  17.1 143.8 %all-gather.11.cloned.1.call-start = ((), (), s32[]{:S(2)}) async-start(), calls=%async_computation.3 | async-start | bytes 2228224 | tf_op jit(solution)/shard_map/all_gather | solution.py:112
  17.9 185.7 %all-gather.5.cloned.1.call-start = ((), (), s32[]{:S(2)}) async-start(), calls=%async_computation | async-start | bytes 2228224 | tf_op jit(solution)/shard_map/all_gather | solution.py:114
  18.6 227.4 %all-gather.7.cloned.1.call-start = ((), (), s32[]{:S(2)}) async-start(), calls=%async_computation.1 | async-start | bytes 2228224 | tf_op jit(solution)/shard_map/all_gather | solution.py:113
  19.2 269.3 %all-gather.9.cloned.1.call-start = ((), (), s32[]{:S(2)}) async-start(), calls=%async_computation.2 | async-start | bytes 2228224 | tf_op jit(solution)/shard_map/all_gather | solution.py:115
  19.8 386.9 %all-reduce.11.cloned.1.call-start = ((), (), s32[]{:S(2)}) async-start(), calls=%async_computation.5 | async-start | bytes 4194304 | tf_op jit(solution)/shard_map/psum | solution.py:136
  295.0 8.5 %copy-start.6 = (s32[1,64]{1,0:T(1,128)S(1)}, s32[1,64]{1,0:T(1,128)}, u32[]{:S(2)}) copy-start(s32[1,64]{1,0:T(1,128)} %param.16) | copy-start | bytes 772
  295.1 8.5 %copy-start.10 = (f32[1,8,128]{2,1,0:T(8,128)S(1)}, f32[1,8,128]{2,1,0:T(8,128)}, u32[]{:S(2)}) copy-start(f32[1,8,128]{2,1,0:T(8,128)} %param.26) | copy-start | bytes 12292
  295.1 8.8 %copy-start.5 = (f32[1,8,128]{2,1,0:T(8,128)S(1)}, f32[1,8,128]{2,1,0:T(8,128)}, u32[]{:S(2)}) copy-start(f32[1,8,128]{2,1,0:T(8,128)} %param.29) | copy-start | bytes 12292
  295.1 9.0 %copy-start.1 = (f32[1,64,128,128]{3,2,1,0:T(8,128)S(1)}, f32[1,64,128,128]{3,2,1,0:T(8,128)}, u32[]{:S(2)}) copy-start(f32[1,64,128,128]{3,2,1,0:T(8,128)} %param.15) | copy-start | bytes 12582916
  307.7 99.0 %copy-start.3 = (f32[4096,128]{1,0:T(8,128)S(1)}, f32[4096,128]{1,0:T(8,128)}, u32[]{:S(2)}) copy-start(f32[4096,128]{1,0:T(8,128)} %all-gather.11.cloned.1.call-done) | copy-start | bytes 6291460
  310.0 217.3 %all-reduce.13.cloned.1.call-start = ((), (), s32[]{:S(2)}) async-start(), calls=%async_computation.6 | async-start | bytes 4194304 | tf_op jit(solution)/shard_map/psum | solution.py:136
  415.2 9.0 %copy-start.2 = (f32[1,64,128,128]{3,2,1,0:T(8,128)S(1)}, f32[1,64,128,128]{3,2,1,0:T(8,128)}, u32[]{:S(2)}) copy-start(f32[1,64,128,128]{3,2,1,0:T(8,128)} %param.15) | copy-start | bytes 12582916
Sparse Core Ops, SparseCore 0:
  17.2 100.5 all-reduce.8
  120.3 40.6 all-gather.10
  163.3 40.1 all-gather.4
  205.8 40.1 all-gather.6
  248.2 40.1 all-gather.8
  310.2 96.5 all-reduce.10
  430.3 97.0 all-reduce.12
where the time goes:
time: 588 us
  waiting for transfers between devices  407 us (69%)
  blocking collectives  81.2 us (14%)
  matrix products  41.5 us (7%)
  other arithmetic  31.8 us (5%)
  between operations  16.3 us (3%)
  local copies, waits for them, and re-layouts  9.54 us (2%)
    psum x3, waiting for transfers between devices, shards(): grad_first = lax.psum(grad_first_part, ('scen', 'blk', 'sub'))  234 us
    all_gather x1, waiting for transfers between devices, shards(): lax.all_gather(cost_first, ('scen', 'blk', 'sub'), axis=0, tiled=True)  43.1 us
    all_gather x1, waiting for transfers between devices, shards(): lax.all_gather(upper_first, ('scen', 'blk', 'sub'), axis=0, tiled=True)  42.6 us
    all_gather x1, waiting for transfers between devices, shards(): lax.all_gather(lower_first, ('scen', 'blk', 'sub'), axis=0, tiled=True)  42.5 us
    all_gather x1, waiting for transfers between devices, shards(): lax.all_gather(first_start, ('scen', 'blk', 'sub'), axis=0, tiled=True)  42.4 us
    unnamed x3, blocking collectives  34.2 us
    psum x1, blocking collectives, shards(): squares.append(lax.psum(local_square, ('scen', 'blk', 'sub')))  31.1 us
    dot_general x3, matrix products, forward_window(): jnp.einsum('skij,skj->ski', block_matrices, blocks, precision=precise)  25.2 us
  transfers between devices with their start and end apart: 7, of which 7 were waited for; matrix products, arithmetic and copies ran while one was open for 1% of the time, Pallas kernels for 0%

commit v1 on v0

--- a/solution.py
+++ b/solution.py
@@ -133,7 +133,7 @@
         grad_second = lax.psum_scatter(
             grad_second_part, ("blk", "sub"), scatter_dimension=1, tiled=True
         )
-        grad_first = lax.psum(grad_first_part, ("scen", "blk", "sub"))
+        grad_first = jnp.sum(lax.all_gather(grad_first_part, ("scen", "blk", "sub")), axis=0)
         first_next = jnp.clip(
             first_now - step_primal * (cost_all - grad_first), lower_all, upper_all
         )

time: 588 us -> 830 us (1.41)
  waiting for transfers between devices: 407 us -> 605 us
  other arithmetic: 31.8 us -> 69.9 us
    all_gather x0 -> x3, waiting for transfers between devices: none -> 444 us  [shards(): lax.all_gather(grad_first_part, ('scen', 'blk', 'sub'))]
    psum x3 -> x0, waiting for transfers between devices: 234 us -> none  [shards(): grad_first = lax.psum(grad_first_part, ('scen', 'blk', 'sub'))]
    reduce_sum x0 -> x3, other arithmetic: none -> 38.1 us  [shards(): jnp.sum(lax.all_gather(grad_first_part, ('scen', 'blk', 'sub')), axis=0)]
    all_gather x1, waiting for transfers between devices: 42.6 us -> 32.1 us  [shards(): lax.all_gather(upper_first, ('scen', 'blk', 'sub'), axis=0, tiled=True)]
  transfers between devices with their start and end apart: 7 -> 7, of which waited for: 7 -> 7; matrix products, arithmetic and copies ran while one was open for 1% -> 2% of each run, Pallas kernels for 0% -> 0%
where the time goes in v1:
time: 830 us
  waiting for transfers between devices  605 us (73%)
  blocking collectives  85 us (10%)
  other arithmetic  69.9 us (8%)
  matrix products  41.8 us (5%)
  between operations  16.4 us (2%)
  local copies, waits for them, and re-layouts  11.1 us (1%)
    all_gather x3, waiting for transfers between devices, shards(): lax.all_gather(grad_first_part, ('scen', 'blk', 'sub'))  444 us
    all_gather x1, waiting for transfers between devices, shards(): lax.all_gather(lower_first, ('scen', 'blk', 'sub'), axis=0, tiled=True)  42.4 us
    all_gather x1, waiting for transfers between devices, shards(): lax.all_gather(cost_first, ('scen', 'blk', 'sub'), axis=0, tiled=True)  42.2 us
    all_gather x1, waiting for transfers between devices, shards(): lax.all_gather(first_start, ('scen', 'blk', 'sub'), axis=0, tiled=True)  42.2 us
    reduce_sum x3, other arithmetic, shards(): jnp.sum(lax.all_gather(grad_first_part, ('scen', 'blk', 'sub')), axis=0)  38.1 us
    unnamed x3, blocking collectives  35.8 us
    psum x1, blocking collectives, shards(): squares.append(lax.psum(local_square, ('scen', 'blk', 'sub')))  33.4 us
    all_gather x1, waiting for transfers between devices, shards(): lax.all_gather(upper_first, ('scen', 'blk', 'sub'), axis=0, tiled=True)  32.1 us
  transfers between devices with their start and end apart: 7, of which 7 were waited for; matrix products, arithmetic and copies ran while one was open for 2% of the time, Pallas kernels for 0%

profile of v1, /device:TPU:0, one launch (start us, length us, event | category | flops | bytes accessed | tf_op | source)
XLA Modules:
  0.0 829.7 jit_solution(3357280426610749607)
XLA Ops:
  9.5 5.3 fusion.10
  22.6 13.4 %all-reduce.1 = f32[1,32,128]{2,1,0:T(8,128)S(1)} all-reduce(f32[1,32,128]{2,1,0:T(8,128)S(1)} %bitcast.141), channel_id=5, replica_groups=mesh['grp'=2,'scen'=4,'blk'=2,'sub'=2] {'blk','sub'}, use_global_device_ids=true, to_apply=%region_3.4.clone | all-reduce | flops 4096 | bytes 32768
  36.2 5.2 all_gather.45
  42.3 145.7 %all-gather.19.cloned.1.call-done = f32[65536,128]{1,0:T(8,128)} async-done(((f32[4096,128]{1,0:T(8,128)}), f32[65536,128]{1,0:T(8,128)}) %all-gather.19.cloned.1.call-update) | async-done | bytes 33554448 | tf_op jit(solution)/shard_map/all_gather | solution.py:136
  188.0 11.8 %reduce_sum.54 = f32[4096,128]{1,0:T(8,128)S(1)} reduce(f32[16,4096,128]{2,1,0:T(8,128)} %bitcast.126, f32[]{:T(128)} %constant.16.clone.1), dimensions={0}, to_apply=%region_1.2 | reduce | flops 7864320 | bytes 35651588 | tf_op jit(solution)/shard_map/reduce_sum | solution.py:136
  199.8 32.1 %all-gather.11.cloned.1.call-done = f32[4096,128]{1,0:T(8,128)} async-done(((f32[256,128]{1,0:T(8,128)}), f32[4096,128]{1,0:T(8,128)}) %all-gather.11.cloned.1.call-update) | async-done | bytes 2097168 | tf_op jit(solution)/shard_map/all_gather | solution.py:114
  232.0 42.4 %all-gather.13.cloned.1.call-done = f32[4096,128]{1,0:T(8,128)} async-done(((f32[256,128]{1,0:T(8,128)}), f32[4096,128]{1,0:T(8,128)}) %all-gather.13.cloned.1.call-update) | async-done | bytes 2097168 | tf_op jit(solution)/shard_map/all_gather | solution.py:113
  274.3 42.2 %all-gather.17.cloned.1.call-done = f32[4096,128]{1,0:T(8,128)} async-done(((f32[256,128]{1,0:T(8,128)}), f32[4096,128]{1,0:T(8,128)}) %all-gather.17.cloned.1.call-update) | async-done | bytes 2097168 | tf_op jit(solution)/shard_map/all_gather | solution.py:112
  316.6 42.2 %all-gather.15.cloned.1.call-done = f32[4096,128]{1,0:T(8,128)} async-done(((f32[256,128]{1,0:T(8,128)}), f32[4096,128]{1,0:T(8,128)}) %all-gather.15.cloned.1.call-update) | async-done | bytes 2097168 | tf_op jit(solution)/shard_map/all_gather | solution.py:115
  358.8 6.0 multiply_subtract_fusion.2
  367.1 8.6 %fusion.8 = f32[64,1,128]{2,1,0:T(1,128)S(1)} fusion(f32[64,128,1]{1,2,0:T(1,128)S(1)} %bitcast.136, f32[1,64,128,128]{3,2,1,0:T(8,128)} %param.15), kind=kOutput, calls=%fused_computation.20 | convolution fusion | flops 12582912 | bytes 4259840 | tf_op jit(solution)/shard_map/skij,skj->ski/dot_general | solution.py:29
  383.4 10.9 %all-reduce.2 = f32[1,32,128]{2,1,0:T(8,128)S(1)} all-reduce(f32[1,32,128]{2,1,0:T(8,128)S(1)} %bitcast.143), channel_id=6, replica_groups=mesh['grp'=2,'scen'=4,'blk'=2,'sub'=2] {'blk','sub'}, use_global_device_ids=true, to_apply=%region_7.8.clone | all-reduce | flops 4096 | bytes 32768
  394.3 5.2 all_gather.48
  400.3 148.9 %all-gather.21.cloned.1.call-done = f32[65536,128]{1,0:T(8,128)} async-done(((f32[4096,128]{1,0:T(8,128)}), f32[65536,128]{1,0:T(8,128)}) %all-gather.21.cloned.1.call-update) | async-done | bytes 33554448 | tf_op jit(solution)/shard_map/all_gather | solution.py:136
  549.3 13.3 %reduce_sum.55 = f32[4096,128]{1,0:T(8,128)} reduce(f32[16,4096,128]{2,1,0:T(8,128)} %bitcast.128, f32[]{:T(128)} %constant.16.clone.1), dimensions={0}, to_apply=%region_5.6 | reduce | flops 7864320 | bytes 35651588 | tf_op jit(solution)/shard_map/reduce_sum | solution.py:136
  562.5 6.1 multiply_subtract_fusion.1
  570.9 8.6 %fusion.4 = f32[64,1,128]{2,1,0:T(1,128)S(1)} fusion(f32[64,128,1]{1,2,0:T(1,128)S(1)} %bitcast.137, f32[1,64,128,128]{3,2,1,0:T(8,128)} %param.15), kind=kOutput, calls=%fused_computation.16 | convolution fusion | flops 12582912 | bytes 4259840 | tf_op jit(solution)/shard_map/skij,skj->ski/dot_general | solution.py:29
  586.8 11.5 %all-reduce.3 = f32[1,32,128]{2,1,0:T(8,128)S(1)} all-reduce(f32[1,32,128]{2,1,0:T(8,128)S(1)} %bitcast.142), channel_id=7, replica_groups=mesh['grp'=2,'scen'=4,'blk'=2,'sub'=2] {'blk','sub'}, use_global_device_ids=true, to_apply=%region_11.12.clone | all-reduce | flops 4096 | bytes 32768
  598.9 5.4 all_gather.51
  605.2 149.2 %all-gather.23.cloned.1.call-done = f32[65536,128]{1,0:T(8,128)} async-done(((f32[4096,128]{1,0:T(8,128)}), f32[65536,128]{1,0:T(8,128)}) %all-gather.23.cloned.1.call-update) | async-done | bytes 33554448 | tf_op jit(solution)/shard_map/all_gather | solution.py:136
  754.3 13.0 %reduce_sum.56 = f32[4096,128]{1,0:T(8,128)} reduce(f32[16,4096,128]{2,1,0:T(8,128)} %bitcast.127, f32[]{:T(128)} %constant.16.clone.1), dimensions={0}, to_apply=%region_9.10 | reduce | flops 7864320 | bytes 35651588 | tf_op jit(solution)/shard_map/reduce_sum | solution.py:136
  767.4 6.0 multiply_subtract_fusion
  775.6 8.3 %fusion = f32[64,1,128]{2,1,0:T(1,128)S(1)} fusion(f32[64,128,1]{1,2,0:T(1,128)S(1)} %bitcast.135, f32[1,64,128,128]{3,2,1,0:T(8,128)} %param.15), kind=kOutput, calls=%fused_computation.12 | convolution fusion | flops 12582912 | bytes 4259840 | tf_op jit(solution)/shard_map/skij,skj->ski/dot_general | solution.py:29
  787.0 33.4 %all-reduce.4 = (f32[1]{0:T(128)}, f32[1]{0:T(128)}, f32[1]{0:T(128)}) all-reduce(f32[1]{0:T(128)} %bitcast.57, f32[1]{0:T(128)} %bitcast.56, f32[1]{0:T(128)} %bitcast.55), channel_id=1, replica_groups=mesh['grp'=2,'scen'=4,'blk'=2,'sub'=2] {'scen','blk','sub'}, use_global_device_ids=true, to_apply=%region_17.18 | all-reduce | flops 3 | bytes 24 | tf_op jit(solution)/shard_map/psum | solution.py:159
  (79 shorter events, 38.5 us)
Async XLA Ops:
  7.2 28.8 %copy-start = (f32[24,8,128]{2,1,0:T(8,128)S(1)}, f32[24,8,128]{2,1,0:T(8,128)}, u32[]{:S(2)}) copy-start(f32[24,8,128]{2,1,0:T(8,128)} %param.20) | copy-start | bytes 294916
  7.2 180.8 %all-gather.19.cloned.1.call-start = ((), (), s32[]{:S(2)}) async-start(), calls=%async_computation.4 | async-start | bytes 35651584 | tf_op jit(solution)/shard_map/all_gather | solution.py:136
  14.8 5.0 copy-start.10
  14.8 6.6 copy-start.12
  14.8 21.4 %copy-start.5 = (f32[1,8,128]{2,1,0:T(8,128)S(1)}, f32[1,8,128]{2,1,0:T(8,128)}, u32[]{:S(2)}) copy-start(f32[1,8,128]{2,1,0:T(8,128)} %param.25) | copy-start | bytes 12292
  14.8 21.4 %copy-start.8 = (f32[1,8,128]{2,1,0:T(8,128)S(1)}, f32[1,8,128]{2,1,0:T(8,128)}, u32[]{:S(2)}) copy-start(f32[1,8,128]{2,1,0:T(8,128)} %param.28) | copy-start | bytes 12292
  14.8 21.4 %copy-start.9 = (f32[1,8,128]{2,1,0:T(8,128)S(1)}, f32[1,8,128]{2,1,0:T(8,128)}, u32[]{:S(2)}) copy-start(f32[1,8,128]{2,1,0:T(8,128)} %param.24) | copy-start | bytes 12292
  17.1 214.9 %all-gather.11.cloned.1.call-start = ((), (), s32[]{:S(2)}) async-start(), calls=%async_computation | async-start | bytes 2228224 | tf_op jit(solution)/shard_map/all_gather | solution.py:114
  17.8 256.5 %all-gather.13.cloned.1.call-start = ((), (), s32[]{:S(2)}) async-start(), calls=%async_computation.1 | async-start | bytes 2228224 | tf_op jit(solution)/shard_map/all_gather | solution.py:113
  18.6 298.0 %all-gather.17.cloned.1.call-start = ((), (), s32[]{:S(2)}) async-start(), calls=%async_computation.3 | async-start | bytes 2228224 | tf_op jit(solution)/shard_map/all_gather | solution.py:112
  19.1 339.6 %all-gather.15.cloned.1.call-start = ((), (), s32[]{:S(2)}) async-start(), calls=%async_computation.2 | async-start | bytes 2228224 | tf_op jit(solution)/shard_map/all_gather | solution.py:115
  19.7 529.5 %all-gather.21.cloned.1.call-start = ((), (), s32[]{:S(2)}) async-start(), calls=%async_computation.5 | async-start | bytes 35651584 | tf_op jit(solution)/shard_map/all_gather | solution.py:136
  367.1 8.7 %copy-start.7 = (s32[1,64]{1,0:T(1,128)S(1)}, s32[1,64]{1,0:T(1,128)}, u32[]{:S(2)}) copy-start(s32[1,64]{1,0:T(1,128)} %param.16) | copy-start | bytes 772
  367.1 8.7 %copy-start.11 = (f32[1,8,128]{2,1,0:T(8,128)S(1)}, f32[1,8,128]{2,1,0:T(8,128)}, u32[]{:S(2)}) copy-start(f32[1,8,128]{2,1,0:T(8,128)} %param.26) | copy-start | bytes 12292
  367.1 8.9 %copy-start.6 = (f32[1,8,128]{2,1,0:T(8,128)S(1)}, f32[1,8,128]{2,1,0:T(8,128)}, u32[]{:S(2)}) copy-start(f32[1,8,128]{2,1,0:T(8,128)} %param.29) | copy-start | bytes 12292
  367.1 9.1 %copy-start.2 = (f32[1,64,128,128]{3,2,1,0:T(8,128)S(1)}, f32[1,64,128,128]{3,2,1,0:T(8,128)}, u32[]{:S(2)}) copy-start(f32[1,64,128,128]{3,2,1,0:T(8,128)} %param.15) | copy-start | bytes 12582916
  382.3 372.1 %all-gather.23.cloned.1.call-start = ((), (), s32[]{:S(2)}) async-start(), calls=%async_computation.6 | async-start | bytes 35651584 | tf_op jit(solution)/shard_map/all_gather | solution.py:136
  549.3 13.3 %copy-start.4 = (f32[4096,128]{1,0:T(8,128)S(1)}, f32[4096,128]{1,0:T(8,128)}, u32[]{:S(2)}) copy-start(f32[4096,128]{1,0:T(8,128)} %all-gather.11.cloned.1.call-done) | copy-start | bytes 6291460
  570.9 9.1 %copy-start.3 = (f32[1,64,128,128]{3,2,1,0:T(8,128)S(1)}, f32[1,64,128,128]{3,2,1,0:T(8,128)}, u32[]{:S(2)}) copy-start(f32[1,64,128,128]{3,2,1,0:T(8,128)} %param.15) | copy-start | bytes 12582916
  775.6 47.3 %copy-start.1 = (f32[24,8,128]{2,1,0:T(8,128)S(1)}, f32[24,8,128]{2,1,0:T(8,128)}, u32[]{:S(2)}) copy-start(f32[24,8,128]{2,1,0:T(8,128)} %param.20) | copy-start | bytes 294916
Sparse Core Ops, SparseCore 0:
  17.2 170.7 all-gather.18
  190.2 41.7 all-gather.10
  234.1 40.1 all-gather.12
  276.4 40.1 all-gather.16
  318.6 40.1 all-gather.14
  382.4 166.8 all-gather.20
  586.1 168.2 all-gather.22
